TPU v7x, 256 devices: a whole 4x4x8 slice. The times are simulated.
256 devices in a mesh: leaf: 16 (over z, core), group: 16 (over x, y).
Axes of the slice: x: 4, y: 4, z: 8, core: 2. Of those that a mesh axis runs over, the one named last changes fastest.
Arguments:
- tile_fields: bfloat16 [2048, 32, 32, 512], P(('leaf', 'group')), may hold values from -2500 to 2500
- routes: int32 [256, 8], P(('leaf', 'group')), may hold values from 0 to 15, as said below
- counts: int32 [256], P(('leaf', 'group')), may hold values from 5 to 8
Outputs:
- factor: float32 [16, 16], replicated
- mode_blocks: float32 [4096, 256, 256], P(('leaf', 'group'))
Inputs may be any that keep to these rules, and one draw needn't show every extreme that they name: `routes`: the 8 entries of a device are distinct. In every group some leaf index is named by an occupied slot of every device of the group, and every leaf index is named by an occupied slot of some device of the group.
All inputs are finite; a program needn't handle non-finite values.
Results may differ from a plain program's by a relative error of at most 0.012.
The roundings to bfloat16 on the way count: a program that leaves them out, or rounds other values in their place, can miss the bound.
Values may be sent and summed in bfloat16 or wider, within the bound.
A program may use at most 128 MiB of HBM per device.

v0:
```python
import jax
import jax.numpy as jnp
from jax import lax
from jax.sharding import PartitionSpec as P


def smoother(length):
    half_edge = length // 2
    row_index = jnp.arange(half_edge)[:, None]
    col_index = jnp.arange(length)[None, :]
    offset = (col_index - 2 * row_index).astype(jnp.float32)
    tap_offsets = jnp.arange(-4, 5).astype(jnp.float32)
    normalizer = jnp.sum(jnp.exp(-tap_offsets * tap_offsets / 4.5))
    weights = jnp.where(jnp.abs(offset) <= 4.0, jnp.exp(-offset * offset / 4.5) / normalizer, 0.0)
    return weights.astype(jnp.bfloat16)


def cholesky_upper(gram):
    order = gram.shape[0]
    positions = jnp.arange(order)
    upper = jnp.zeros_like(gram)
    for row_index in range(order):
        partial_row = gram[row_index] - jnp.sum(upper[:, row_index][:, None] * upper, axis=0)
        pivot = jnp.sqrt(partial_row[row_index])
        new_row = jnp.where(
            positions >= row_index, partial_row / pivot, jnp.zeros_like(partial_row)
        )
        upper = upper.at[row_index].set(new_row)
    return upper


def invert_upper(upper):
    order = upper.shape[0]
    positions = jnp.arange(order)
    identity = jnp.eye(order, dtype=upper.dtype)
    result = jnp.zeros_like(upper)
    for row_index in range(order - 1, -1, -1):
        off_diagonal = jnp.where(
            positions > row_index, upper[row_index], jnp.zeros_like(upper[row_index])
        )
        partial_row = identity[row_index] - jnp.sum(off_diagonal[:, None] * result, axis=0)
        result = result.at[row_index].set(partial_row / upper[row_index, row_index])
    return result


def filter_tiles(payload):
    slots_here = payload.shape[0]
    tile_edge = payload.shape[1]
    half_edge = tile_edge // 2
    snapshots = payload.shape[3] // tile_edge
    weights = smoother(tile_edge)
    first_pass = jnp.einsum(
        "ix,sxr->sir",
        weights,
        payload.reshape(slots_here, tile_edge, tile_edge * tile_edge * snapshots),
        preferred_element_type=jnp.float32,
    ).astype(jnp.bfloat16)
    second_pass = jnp.einsum(
        "jy,siyc->sijc",
        weights,
        first_pass.reshape(slots_here, half_edge, tile_edge, tile_edge * snapshots),
        preferred_element_type=jnp.float32,
    ).astype(jnp.bfloat16)
    depth_table = jnp.kron(weights, jnp.eye(snapshots, dtype=jnp.bfloat16))
    flat_second = second_pass.reshape(slots_here * half_edge * half_edge, tile_edge * snapshots)
    third_pass = lax.dot_general(
        flat_second, depth_table, (((1,), (1,)), ((), ())), preferred_element_type=jnp.float32
    ).astype(jnp.bfloat16)
    return third_pass.reshape(slots_here, half_edge * half_edge, half_edge * snapshots)


def gram_matrix(filtered, snapshots):
    flat_rows = filtered.reshape(-1, filtered.shape[-1] // snapshots, snapshots)
    return lax.dot_general(
        flat_rows, flat_rows, (((0, 1), (0, 1)), ((), ())), preferred_element_type=jnp.float32
    )


def place_tiles(payload, route_row, count_here, leaves):
    buffer = jnp.zeros((leaves,) + payload.shape[1:], payload.dtype)
    for slot_index in range(payload.shape[0]):
        tile_piece = jnp.where(
            slot_index < count_here, payload[slot_index], jnp.zeros_like(payload[slot_index])
        )
        buffer = lax.dynamic_update_slice_in_dim(buffer, tile_piece[None], route_row[slot_index], 0)
    return buffer


def shards(tile_fields, routes, counts):
    leaves = lax.axis_size("leaf")
    groups = lax.axis_size("group")
    slots_here = tile_fields.shape[0]
    tile_edge = tile_fields.shape[1]
    snapshots = tile_fields.shape[3] // tile_edge
    half_edge = tile_edge // 2
    rows_all = half_edge**3 * slots_here * leaves * groups
    route_row = routes[0]
    count_here = counts[0]
    incoming = lax.all_to_all(
        place_tiles(tile_fields, route_row, count_here, leaves),
        "leaf",
        split_axis=0,
        concat_axis=0,
        tiled=True,
    )
    arrived = filter_tiles(incoming)
    local_gram = gram_matrix(arrived, snapshots)
    summed = lax.psum(local_gram, ("leaf", "group"))
    factor = cholesky_upper(summed / rows_all)
    inverse = invert_upper(factor)
    block_inverse = jnp.kron(jnp.eye(half_edge, dtype=jnp.float32), inverse)
    flat_rows = arrived.reshape(leaves * half_edge * half_edge, half_edge * snapshots).astype(
        jnp.float32
    )
    mode_blocks = jnp.dot(flat_rows, block_inverse, precision=lax.Precision.HIGHEST)
    return (factor, mode_blocks.reshape(leaves, half_edge * half_edge, half_edge * snapshots))


def solution(mesh):
    return jax.shard_map(
        shards,
        mesh=mesh,
        in_specs=(
            P(("leaf", "group"), None, None, None),
            P(("leaf", "group"), None),
            P(("leaf", "group")),
        ),
        out_specs=(P(), P(("leaf", "group"), None, None)),
        check_vma=False,
    )
```

profile of v0, /device:TPU:1, one launch (start us, length us, event | category | flops | bytes accessed | tf_op | source)
XLA Modules:
  0.0 622.4 jit_solution(9531453409262674630)
XLA Ops:
  0.6 1.6 fusion.44
  18.1 8.0 %broadcast_in_dim.9 = bf16[16,32,32,512]{3,2,1,0:T(8,128)(2,1)} broadcast(bf16[]{:T(256)} %constant.803.clone.1), dimensions={} | broadcast | bytes 16777218 | tf_op jit(solution)/shard_map/broadcast_in_dim | solution.py:80
  26.4 1.2 select_dynamic-update-slice_fusion.7
  27.6 1.3 select_dynamic-update-slice_fusion.6
  28.9 1.2 select_dynamic-update-slice_fusion.5
  30.2 1.2 select_dynamic-update-slice_fusion.4
  31.4 1.2 select_dynamic-update-slice_fusion.3
  32.6 1.2 select_dynamic-update-slice_fusion.2
  33.8 1.2 select_dynamic-update-slice_fusion.1
  35.0 1.3 select_dynamic-update-slice_fusion
  36.3 9.8 %all-to-all-start = ((bf16[16,32,32,512]{3,2,1,0:T(8,128)(2,1)}), bf16[16,32,32,512]{3,2,1,0:T(8,128)(2,1)}, u32[]{:S(2)}, u32[]{:S(2)}) async-start(bf16[16,32,32,512]{3,2,1,0:T(8,128)(2,1)} %select_dynamic-update-slice_fusion), calls=%async_computation | async-start | bytes 33554432 | tf_op jit(solution)/shard_map/all_to_all | solution.py:99
  46.8 0.7 fusion.11
  47.7 3.6 mul.363
  51.3 357.9 %all-to-all-done = bf16[16,32,32,512]{3,2,1,0:T(8,128)(2,1)} async-done(((bf16[16,32,32,512]{3,2,1,0:T(8,128)(2,1)}), bf16[16,32,32,512]{3,2,1,0:T(8,128)(2,1)}, u32[]{:S(2)}, u32[]{:S(2)}) %all-to-all-start) | async-done | bytes 16777248 | tf_op jit(solution)/shard_map/all_to_all | solution.py:99
  409.2 25.6 %reshape.1109 = bf16[16,32,16384]{2,1,0:T(8,128)(2,1)} reshape(bf16[16,32,32,512]{3,2,1,0:T(8,128)(2,1)} %all-to-all-done) | data formatting | bytes 33554432 | tf_op jit(solution)/shard_map/reshape | solution.py:55
  434.8 12.1 %convolution_convert_fusion = bf16[16,16384,16]{1,2,0:T(8,128)(2,1)} fusion(bf16[16,32,16384]{2,1,0:T(8,128)(2,1)} %reshape.1109, f32[]{:T(128)} %fusion.18, s32[16]{0:T(128)S(1)} %iota_multiply_fusion), kind=kOutput, calls=%fused_computation | convolution fusion | flops 272634880 | bytes 25165892 | tf_op jit(solution)/shard_map/ix,sxr->sir/dot_general | solution.py:52
  446.9 10.4 %copy.9 = bf16[32,8,32,512]{3,2,1,0:T(8,128)(2,1)} copy(bf16[32,8,32,512]{3,1,2,0:T(8,128)(2,1)} %bitcast.268) | data formatting | bytes 16777216
  457.3 5.3 fusion.2
  462.6 2.6 convolution_convert_fusion.1
  465.3 2.9 copy.7
  468.2 1.0 convolution_bitcast_fusion
  469.2 77.9 %psum.7 = f32[16,16]{1,0:T(8,128)S(1)} all-reduce(f32[16,16]{1,0:T(8,128)S(1)} %convolution_bitcast_fusion), channel_id=1, replica_groups=mesh['leaf'=16,'group'=16] {'leaf','group'}, use_global_device_ids=true, to_apply=%region_1.2 | all-reduce | flops 256 | bytes 2048 | tf_op jit(solution)/shard_map/psum | solution.py:108
  552.1 0.7 compare_select_fusion.30
  553.1 0.7 bitcast_subtract_fusion.24
  555.1 0.7 compare_select_fusion.29
  556.1 0.7 bitcast_subtract_fusion.22
  558.0 0.7 compare_select_fusion.28
  559.0 0.7 bitcast_subtract_fusion.20
  562.0 0.7 bitcast_subtract_fusion.18
  563.9 0.7 compare_select_fusion.26
  564.9 0.7 bitcast_subtract_fusion.16
  569.8 0.7 compare_select_fusion.24
  570.8 0.7 bitcast_subtract_fusion.12
  572.8 0.7 compare_select_fusion.23
  573.8 0.7 bitcast_subtract_fusion.10
  575.7 0.7 compare_select_fusion.22
  576.7 0.7 bitcast_subtract_fusion.8
  578.7 0.7 compare_select_fusion.21
  579.7 0.7 bitcast_subtract_fusion.6
  581.6 0.7 compare_select_fusion.20
  582.6 0.7 bitcast_subtract_fusion.4
  584.6 0.7 compare_select_fusion.19
  585.6 0.7 bitcast_subtract_fusion.2
  587.5 0.7 compare_select_fusion.18
  588.5 0.7 bitcast_subtract_fusion
  592.5 0.7 fusion.43
  593.2 1.2 fusion.35
  595.2 1.3 fusion.33
  596.6 1.3 fusion.32
  598.0 1.2 fusion.31
  599.4 1.4 fusion.30
  600.9 1.4 fusion.29
  602.4 1.3 fusion.28
  603.8 1.3 fusion.27
  605.2 1.4 fusion.26
  606.7 1.4 fusion.25
  608.2 1.3 fusion.24
  609.6 1.3 fusion.23
  611.0 1.3 fusion.22
  612.5 1.2 fusion.21
  613.8 1.3 fusion.20
  615.2 0.9 broadcast_multiply_fusion
  616.1 0.9 reshape.1115
  617.0 5.4 fusion.45
  (117 shorter events, 22.2 us)
Async XLA Ops:
  18.1 8.4 %copy-start = (bf16[8,32,32,512]{3,2,1,0:T(8,128)(2,1)S(1)}, bf16[8,32,32,512]{3,2,1,0:T(8,128)(2,1)}, u32[]{:S(2)}) copy-start(bf16[8,32,32,512]{3,2,1,0:T(8,128)(2,1)} %param.67) | copy-start | bytes 25165828
  36.3 372.9 %all-to-all-start = ((bf16[16,32,32,512]{3,2,1,0:T(8,128)(2,1)}), bf16[16,32,32,512]{3,2,1,0:T(8,128)(2,1)}, u32[]{:S(2)}, u32[]{:S(2)}) async-start(bf16[16,32,32,512]{3,2,1,0:T(8,128)(2,1)} %select_dynamic-update-slice_fusion), calls=%async_computation | async-start | bytes 33554432 | tf_op jit(solution)/shard_map/all_to_all | solution.py:99
  51.3 543.2 %copy-start.2 = (f32[16,16]{1,0:T(8,128)}, f32[16,16]{1,0:T(8,128)S(1)}, u32[]{:S(2)}) copy-start(f32[16,16]{1,0:T(8,128)S(1)} %fusion.9) | copy-start | bytes 3076
  547.1 3.1 copy-start.3
  592.4 30.0 %copy-start.1 = (f32[16,16]{1,0:T(8,128)}, f32[16,16]{1,0:T(8,128)S(1)}, u32[]{:S(2)}) copy-start(f32[16,16]{1,0:T(8,128)S(1)} %scatter.131) | copy-start | bytes 3076
where the time goes:
time: 625 us; the launch traced here: 622 us
  waiting for transfers between devices  358 us (57%)
  blocking collectives  77.9 us (12%)
  local copies, waits for them, and re-layouts  67.7 us (11%)
  other arithmetic  55.4 us (9%)
  between operations  27.2 us (4%)
  matrix products  26.4 us (4%)
  starting transfers between devices  9.84 us (2%)
    all_to_all x1, waiting for transfers between devices, shards(): lax.all_to_all(place_tiles(tile_fields, route_row, count_here, leaves), '...  358 us
    psum x1, blocking collectives, shards(): summed = lax.psum(local_gram, ('leaf', 'group'))  77.9 us
    reshape x1, local copies, waits for them, and re-layouts, filter_tiles(): payload.reshape(slots_here, tile_edge, tile_edge * tile_edge * snapshots)  25.6 us
    div x16, other arithmetic, invert_upper(): result = result.at[row_index].set(partial_row / upper[row_index, row_index])  20.2 us
  transfers between devices with their start and end apart: 1, of which 1 were waited for; matrix products, arithmetic and copies ran while one was open for 1% of the time, Pallas kernels for 0%

commit v1 on v0

v1 whole, which is shorter than its diff:
```python
import functools

import jax
import jax.numpy as jnp
import ml_dtypes
import numpy as np
from jax import lax
from jax.experimental import pallas as pl
from jax.experimental.pallas import tpu as pltpu
from jax.sharding import PartitionSpec as P

MESH = pl.DeviceIdType.MESH
F32 = jnp.float32
BF16 = jnp.bfloat16


def smoother(length):
    half_edge = length // 2
    row_index = np.arange(half_edge)[:, None]
    col_index = np.arange(length)[None, :]
    offset = (col_index - 2 * row_index).astype(np.float32)
    tap_offsets = np.arange(-4, 5).astype(np.float32)
    normalizer = np.sum(np.exp(-tap_offsets * tap_offsets / np.float32(4.5)), dtype=np.float32)
    taps = np.exp(-offset * offset / np.float32(4.5)) / normalizer
    weights = np.where(np.abs(offset) <= 4.0, taps, np.float32(0.0))
    return weights.astype(ml_dtypes.bfloat16).astype(np.float32)


def filter_tables(edge, snapshots):
    weights = smoother(edge)
    half = edge // 2
    table_x = np.kron(weights, np.eye(half, dtype=np.float32))
    table_y = np.stack(
        [np.kron(np.eye(half, dtype=np.float32), weights[:, h * half : (h + 1) * half]) for h in range(2)]
    )
    table_z = np.kron(weights.T, np.eye(snapshots, dtype=np.float32))
    as_bf16 = lambda a: a.astype(ml_dtypes.bfloat16)
    return as_bf16(table_x), as_bf16(table_y), as_bf16(table_z)


def dot(a, b):
    return jnp.dot(a, b, preferred_element_type=F32)


def filter_tile(tile, table_x, table_y, table_z):
    edge = tile.shape[0]
    half = edge // 2
    width = tile.shape[2]
    second = None
    for h in range(2):
        rows = tile[:, h * half : (h + 1) * half, :].reshape(edge * half, width)
        first = dot(table_x[...], rows).astype(BF16)
        term = dot(table_y[h], first)
        second = term if second is None else second + term
    return dot(second.astype(BF16), table_z[...]).astype(BF16)


def fold_gram(gram, snapshots):
    size = gram.shape[0]
    rows = lax.broadcasted_iota(jnp.int32, gram.shape, 0) // snapshots
    cols = lax.broadcasted_iota(jnp.int32, gram.shape, 1) // snapshots
    kept = jnp.where(rows == cols, gram, 0.0)
    strip = jnp.sum(kept.reshape(size // snapshots, snapshots, size), axis=0)
    folded = strip[:, :128]
    for start in range(128, size, 128):
        folded = folded + strip[:, start : start + 128]
    shift = 64
    while shift >= snapshots:
        folded = folded + pltpu.roll(folded, shift, axis=1)
        shift //= 2
    return folded


def factor_and_inverse(gram):
    order = gram.shape[0]
    rows = lax.broadcasted_iota(jnp.int32, gram.shape, 0)
    cols = lax.rem(lax.broadcasted_iota(jnp.int32, gram.shape, 1), order)
    rest = gram
    upper = jnp.zeros_like(gram)
    columns = []
    pivots = []
    for r in range(order):
        pivot = jnp.sqrt(rest[r : r + 1, r : r + 1])
        row = jnp.where(cols[:1] >= r, rest[r : r + 1, :] / pivot, 0.0)
        column = jnp.where(rows[:, :1] >= r, rest[:, r : r + 1] / pivot, 0.0)
        upper = jnp.where(rows == r, row, upper)
        columns.append(column)
        pivots.append(pivot)
        rest = rest - column * row
    inverse = jnp.zeros_like(gram)
    for r in range(order - 1, -1, -1):
        beyond = jnp.where(rows[:, :1] > r, columns[r], 0.0)
        unit = jnp.where(cols[:1] == r, 1.0, 0.0)
        row = (unit - jnp.sum(beyond * inverse, axis=0, keepdims=True)) / pivots[r]
        inverse = jnp.where(rows == r, row, inverse)
    return upper, inverse


def all_sum(axis, peers, buffer, send_sems, recv_sems):
    me = lax.axis_index(axis)

    def copy_to(peer):
        return pltpu.make_async_remote_copy(
            src_ref=buffer.at[me],
            dst_ref=buffer.at[me],
            send_sem=send_sems.at[peer],
            recv_sem=recv_sems.at[me],
            device_id={axis: peer},
            device_id_type=MESH,
        )

    def copy_from(peer):
        return pltpu.make_async_remote_copy(
            src_ref=buffer.at[me],
            dst_ref=buffer.at[peer],
            send_sem=send_sems.at[peer],
            recv_sem=recv_sems.at[peer],
            device_id={axis: peer},
            device_id_type=MESH,
        )

    @pl.loop(1, peers)
    def _(step):
        copy_to(lax.rem(me + step, peers)).start()

    @pl.loop(1, peers)
    def _(step):
        copy_from(lax.rem(me + step, peers)).wait_recv()

    total = buffer[0]
    for p in range(1, peers):
        total = total + buffer[p]

    @pl.loop(1, peers)
    def _(step):
        copy_to(lax.rem(me + step, peers)).wait_send()

    return total


def exchange_kernel(
    leaves, groups, snapshots, rows_all, early,
    tiles, routes, counts, table_x, table_y, table_z,
    arrived, factor_out, inverse_out,
    local, outgoing, gram, group_buf, leaf_buf,
    load_sems, self_sem, send_sems, recv_sems, group_send, group_recv, leaf_send, leaf_recv,
):
    slots = tiles.shape[0]
    me = lax.axis_index("leaf")
    my_group = lax.axis_index("group")
    chips = leaves // 2

    def load(t):
        return pltpu.make_async_copy(tiles.at[t], local.at[t], load_sems.at[t])

    for t in range(slots):
        load(t).start()

    barrier = pltpu.get_barrier_semaphore()

    @pl.loop(1, leaves)
    def _(step):
        pl.semaphore_signal(
            barrier, inc=1, device_id={"leaf": lax.rem(me + step, leaves)}, device_id_type=MESH
        )

    @pl.loop(1, groups)
    def _(step):
        pl.semaphore_signal(
            barrier, inc=1, device_id={"group": lax.rem(my_group + step, groups)}, device_id_type=MESH
        )

    gram[...] = jnp.zeros_like(gram)
    for t in range(slots):
        load(t).wait()
    pl.semaphore_wait(barrier, leaves + groups - 2)

    def dest_of(k):
        j = k // 2
        turn = chips // 2 + jnp.where(lax.rem(j, 2) == 0, j // 2, -((j + 1) // 2))
        chip = lax.rem(me // 2 + turn, chips)
        core = lax.rem(lax.rem(me, 2) + lax.rem(k, 2) + 1, 2)
        return chip * 2 + core

    def copy_to(k):
        return pltpu.make_async_remote_copy(
            src_ref=outgoing.at[k],
            dst_ref=arrived.at[me],
            send_sem=send_sems.at[k],
            recv_sem=recv_sems.at[me],
            device_id={"leaf": dest_of(k)},
            device_id_type=MESH,
        )

    def copy_from(source):
        return pltpu.make_async_remote_copy(
            src_ref=outgoing.at[0],
            dst_ref=arrived.at[source],
            send_sem=send_sems.at[0],
            recv_sem=recv_sems.at[source],
            device_id={"leaf": source},
            device_id_type=MESH,
        )

    count = counts[0]

    def prepare(k):
        dest = dest_of(k)
        slot = jnp.int32(0)
        found = jnp.int32(0)
        for t in range(slots):
            hit = jnp.where((routes[0, t] == dest) & (t < count), 1, 0)
            slot = slot + hit * t
            found = found + hit
        block = filter_tile(local[slot], table_x, table_y, table_z)
        block = jnp.where(found > 0, block, jnp.zeros_like(block))
        outgoing[k] = block
        gram[...] += lax.dot_general(
            block, block, (((0,), (0,)), ((), ())), preferred_element_type=F32
        )

    last = leaves - 1

    @pl.loop(0, early)
    def _(k):
        prepare(k)
        copy_to(k).start()

    @pl.loop(early, leaves)
    def _(k):
        prepare(k)

    keep = pltpu.make_async_copy(outgoing.at[last], arrived.at[me], self_sem)
    keep.start()
    group_buf[my_group] = fold_gram(gram[...], snapshots)
    leaf_buf[me] = all_sum("group", groups, group_buf, group_send, group_recv)
    total = all_sum("leaf", leaves, leaf_buf, leaf_send, leaf_recv)

    @pl.loop(early, last)
    def _(k):
        copy_to(k).start()

    upper, inverse = factor_and_inverse(total / rows_all)
    factor_out[...] = upper
    inverse_out[...] = inverse

    keep.wait()

    @pl.loop(1, leaves)
    def _(step):
        copy_from(lax.rem(me + step, leaves)).wait_recv()

    @pl.loop(0, last)
    def _(k):
        copy_to(k).wait_send()


def exchange(tiles, routes, counts, leaves, groups, half, snapshots, rows_all):
    edge = tiles.shape[1]
    slots = tiles.shape[0]
    rows, cols = half * half, half * snapshots
    tables = filter_tables(edge, snapshots)
    vmem = pl.BlockSpec(memory_space=pltpu.VMEM)
    smem = pl.BlockSpec(memory_space=pltpu.SMEM)
    hbm = pl.BlockSpec(memory_space=pl.ANY)
    return pl.pallas_call(
        functools.partial(exchange_kernel, leaves, groups, snapshots, rows_all, 6),
        name="filter_exchange",
        out_shape=(
            jax.ShapeDtypeStruct((leaves, rows, cols), BF16),
            jax.ShapeDtypeStruct((snapshots, 128), F32),
            jax.ShapeDtypeStruct((snapshots, 128), F32),
        ),
        in_specs=[hbm, smem, smem, vmem, vmem, vmem],
        out_specs=(hbm, vmem, vmem),
        scratch_shapes=[
            pltpu.VMEM((slots, edge, edge, edge * snapshots), BF16),
            pltpu.VMEM((leaves, rows, cols), BF16),
            pltpu.VMEM((cols, cols), F32),
            pltpu.VMEM((groups, snapshots, 128), F32),
            pltpu.VMEM((leaves, snapshots, 128), F32),
            pltpu.SemaphoreType.DMA((slots,)),
            pltpu.SemaphoreType.DMA,
            pltpu.SemaphoreType.DMA((leaves,)),
            pltpu.SemaphoreType.DMA((leaves,)),
            pltpu.SemaphoreType.DMA((groups,)),
            pltpu.SemaphoreType.DMA((groups,)),
            pltpu.SemaphoreType.DMA((leaves,)),
            pltpu.SemaphoreType.DMA((leaves,)),
        ],
        compiler_params=pltpu.CompilerParams(
            collective_id=0, has_side_effects=True, vmem_limit_bytes=40 << 20
        ),
    )(tiles, routes, counts, *[jnp.asarray(t) for t in tables])


def apply_kernel(snapshots, blocks, factor, inverse, factor_out, modes, parts):
    @pl.when(pl.program_id(0) == 0)
    def _():
        factor_out[...] = factor[:, :snapshots]
        size = parts.shape[1]
        wide = jnp.concatenate([inverse[...]] * (size // 128), axis=1)
        tall = jnp.concatenate([wide] * (size // snapshots), axis=0)
        rows = lax.broadcasted_iota(jnp.int32, tall.shape, 0) // snapshots
        cols = lax.broadcasted_iota(jnp.int32, tall.shape, 1) // snapshots
        rest = jnp.where(rows == cols, tall, 0.0)
        for p in range(3):
            piece = rest.astype(BF16)
            parts[p] = piece
            rest = rest - piece.astype(F32)

    for b in range(blocks.shape[0]):
        block = blocks[b]
        modes[b] = dot(block, parts[2]) + dot(block, parts[1]) + dot(block, parts[0])


def apply_inverse(blocks, factor, inverse, per_step):
    count, rows, cols = blocks.shape
    snapshots = factor.shape[0]
    whole = lambda shape: pl.BlockSpec(shape, lambda i: (0,) * len(shape))
    step = pl.BlockSpec((per_step, rows, cols), lambda i: (i, 0, 0))
    return pl.pallas_call(
        functools.partial(apply_kernel, snapshots),
        name="apply_inverse",
        out_shape=(
            jax.ShapeDtypeStruct((snapshots, snapshots), F32),
            jax.ShapeDtypeStruct((count, rows, cols), F32),
        ),
        grid=(count // per_step,),
        in_specs=[step, whole(factor.shape), whole(inverse.shape)],
        out_specs=(whole((snapshots, snapshots)), step),
        scratch_shapes=[pltpu.VMEM((3, cols, cols), BF16)],
    )(blocks, factor, inverse)


def shards(tile_fields, routes, counts):
    leaves = lax.axis_size("leaf")
    groups = lax.axis_size("group")
    slots, edge = tile_fields.shape[:2]
    snapshots = tile_fields.shape[3] // edge
    half = edge // 2
    rows_all = half**3 * slots * leaves * groups
    arrived, factor, inverse = exchange(
        tile_fields, routes, counts, leaves, groups, half, snapshots, float(rows_all)
    )
    return apply_inverse(arrived, factor, inverse, 2)


def solution(mesh):
    return jax.shard_map(
        shards,
        mesh=mesh,
        in_specs=(
            P(("leaf", "group"), None, None, None),
            P(("leaf", "group"), None),
            P(("leaf", "group")),
        ),
        out_specs=(P(), P(("leaf", "group"), None, None)),
        check_vma=False,
    )
```

time: 625 us -> 84.9 us (0.14)
  waiting for transfers between devices: 358 us -> 0 us
  blocking collectives: 77.9 us -> 0 us
  Pallas kernels: 0 us -> 73.8 us
  local copies, waits for them, and re-layouts: 67.7 us -> 9.4 us
  other arithmetic: 55.4 us -> 0 us
  matrix products: 26.4 us -> 0 us
  between operations: 27.2 us -> 1.31 us
  starting transfers between devices: 9.84 us -> 0 us
    all_to_all x1 -> x0, waiting for transfers between devices: 358 us -> none  [shards(): lax.all_to_all(place_tiles(tile_fields, route_row, count_here, leaves), '...]
    psum x1 -> x0, blocking collectives: 77.9 us -> none  [shards(): summed = lax.psum(local_gram, ('leaf', 'group'))]
    pallas_call x0 -> x2, Pallas kernels: none -> 73.8 us  [the longest x1 66.4 us: exchange(): pl.pallas_call(functools.partial(exchange_kernel, leaves, groups, snapsho...]
    dot_general x5 -> x0, matrix products: 26.4 us -> none  [the longest x1 12.1 us: filter_tiles(): jnp.einsum('ix,sxr->sir', weights, payload.reshape(slots_here, tile_edge,...]
    reshape x1 -> x0, local copies, waits for them, and re-layouts: 25.6 us -> none  [filter_tiles(): payload.reshape(slots_here, tile_edge, tile_edge * tile_edge * snapshots)]
    div x18 -> x0, other arithmetic: 20.2 us -> none  [the longest x16 20.2 us: invert_upper(): result = result.at[row_index].set(partial_row / upper[row_index, row_index])]
    slice x34 -> x0, local copies, waits for them, and re-layouts: 15.1 us -> none  [the longest x16 9.41 us: cholesky_upper(): pivot = jnp.sqrt(partial_row[row_index])]
    dynamic_update_slice x8 -> x0, other arithmetic: 9.87 us -> none  [place_tiles(): lax.dynamic_update_slice_in_dim(buffer, tile_piece[None], route_row[slot_...]
  transfers between devices with their start and end apart: 1 -> 0, of which waited for: 1 -> 0; matrix products, arithmetic and copies ran while one was open for 1% -> 0% of each run, Pallas kernels for 0% -> 0%
where the time goes in v1:
time: 84.9 us; the launch traced here: 84.5 us
  Pallas kernels  73.8 us (87%)
  local copies, waits for them, and re-layouts  9.4 us (11%)
  between operations  1.31 us (2%)
    pallas_call x1, Pallas kernels, exchange(): pl.pallas_call(functools.partial(exchange_kernel, leaves, groups, snapsho...  66.4 us
    unnamed x16, local copies, waits for them, and re-layouts  9.4 us
    pallas_call x1, Pallas kernels, apply_inverse(): pl.pallas_call(functools.partial(apply_kernel, snapshots), name='apply_in...  7.38 us

profile of v1, /device:TPU:1, one launch (start us, length us, event | category | flops | bytes accessed | tf_op | source)
XLA Modules:
  0.0 84.5 jit_solution(18335931304244975607)
XLA Ops:
  1.3 0.0 copy-start
  1.3 3.4 %copy-done = bf16[8,32,32,512]{3,2,1,0:T(8,128)(2,1)S(1)} copy-done((bf16[8,32,32,512]{3,2,1,0:T(8,128)(2,1)S(1)}, bf16[8,32,32,512]{3,2,1,0:T(8,128)(2,1)}, u32[]{:S(2)}) %copy-start) | copy-done | bytes 8388632
  4.7 0.0 copy-start.2
  4.7 0.9 %copy-done.2 = bf16[512,256]{1,0:T(8,128)(2,1)S(1)} copy-done((bf16[512,256]{1,0:T(8,128)(2,1)S(1)}, bf16[512,256]{1,0:T(8,128)(2,1)}, u32[]{:S(2)}) %copy-start.2) | copy-done | bytes 262168
  5.6 0.0 copy-start.3
  5.6 0.9 %copy-done.3 = bf16[2,256,256]{2,1,0:T(8,128)(2,1)S(1)} copy-done((bf16[2,256,256]{2,1,0:T(8,128)(2,1)S(1)}, bf16[2,256,256]{2,1,0:T(8,128)(2,1)}, u32[]{:S(2)}) %copy-start.3) | copy-done | bytes 262168
  6.6 0.0 copy-start.4
  6.6 0.9 %copy-done.4 = bf16[256,512]{1,0:T(8,128)(2,1)S(1)} copy-done((bf16[256,512]{1,0:T(8,128)(2,1)S(1)}, bf16[256,512]{1,0:T(8,128)(2,1)}, u32[]{:S(2)}) %copy-start.4) | copy-done | bytes 262168
  7.5 0.0 copy-start.7
  7.5 0.7 copy-done.7
  8.2 66.4 %filter_exchange.1 = (bf16[16,256,256]{2,1,0:T(8,128)(2,1)S(1)}, f32[16,128]{1,0:T(8,128)S(1)}, f32[16,128]{1,0:T(8,128)S(1)}) custom-call(bf16[8,32,32,512]{3,2,1,0:T(8,128)(2,1)S(1)} %copy-done, s32[1,8]{1,0:T(1,128)S(1)} %copy-done.7, s32[1]{0:T(128)S(6)} %copy.8.counts, bf16[256,512]{1,0:T(8,128)(2,1)S(1)} %copy-done.4, ...), custom_call_target="tpu_custom_call" | custom-call | tf_op jit(solution)/shard_map/filter_exchange/pallas_call | solution.py:266
  74.6 0.0 copy-start.1
  74.6 1.3 %copy-done.1 = bf16[16,256,256]{2,1,0:T(8,128)(2,1)} copy-done((bf16[16,256,256]{2,1,0:T(8,128)(2,1)}, bf16[16,256,256]{2,1,0:T(8,128)(2,1)S(1)}, u32[]{:S(2)}) %copy-start.1) | copy-done | bytes 2097176
  75.9 0.0 copy-start.5
  75.9 0.6 copy-done.5
  76.5 0.0 copy-start.6
  76.5 0.6 copy-done.6
  77.1 7.4 %apply_inverse.1 = (f32[16,16]{1,0:T(8,128)}, f32[16,256,256]{2,1,0:T(8,128)}) custom-call(bf16[16,256,256]{2,1,0:T(8,128)(2,1)} %copy-done.1, f32[16,128]{1,0:T(8,128)} %copy-done.5, f32[16,128]{1,0:T(8,128)} %copy-done.6), custom_call_target="tpu_custom_call" | custom-call | tf_op jit(solution)/shard_map/apply_inverse/pallas_call | solution.py:322
Async XLA Ops:
  1.3 3.4 %copy-start = (bf16[8,32,32,512]{3,2,1,0:T(8,128)(2,1)S(1)}, bf16[8,32,32,512]{3,2,1,0:T(8,128)(2,1)}, u32[]{:S(2)}) copy-start(bf16[8,32,32,512]{3,2,1,0:T(8,128)(2,1)} %tiles.1) | copy-start | bytes 25165828
  4.7 0.9 %copy-start.2 = (bf16[512,256]{1,0:T(8,128)(2,1)S(1)}, bf16[512,256]{1,0:T(8,128)(2,1)}, u32[]{:S(2)}) copy-start(bf16[512,256]{1,0:T(8,128)(2,1)} %constant.8.clone.table_z) | copy-start | bytes 786436
  5.6 0.9 %copy-start.3 = (bf16[2,256,256]{2,1,0:T(8,128)(2,1)S(1)}, bf16[2,256,256]{2,1,0:T(8,128)(2,1)}, u32[]{:S(2)}) copy-start(bf16[2,256,256]{2,1,0:T(8,128)(2,1)} %constant.7.clone.table_y) | copy-start | bytes 786436
  6.6 0.9 %copy-start.4 = (bf16[256,512]{1,0:T(8,128)(2,1)S(1)}, bf16[256,512]{1,0:T(8,128)(2,1)}, u32[]{:S(2)}) copy-start(bf16[256,512]{1,0:T(8,128)(2,1)} %constant.6.clone.table_x) | copy-start | bytes 786436
  7.5 0.7 copy-start.7
  74.6 1.3 %copy-start.1 = (bf16[16,256,256]{2,1,0:T(8,128)(2,1)}, bf16[16,256,256]{2,1,0:T(8,128)(2,1)S(1)}, u32[]{:S(2)}) copy-start(bf16[16,256,256]{2,1,0:T(8,128)(2,1)S(1)} %get-tuple-element.5.blocks) | copy-start | bytes 6291460
  75.9 0.6 copy-start.5
  76.5 0.6 copy-start.6

commit v2 on v1

v2 whole, which is shorter than its diff:
```python
import functools

import jax
import jax.numpy as jnp
import ml_dtypes
import numpy as np
from jax import lax
from jax.experimental import pallas as pl
from jax.experimental.pallas import tpu as pltpu
from jax.sharding import PartitionSpec as P

MESH = pl.DeviceIdType.MESH
F32 = jnp.float32
BF16 = jnp.bfloat16


def smoother(length):
    half_edge = length // 2
    row_index = np.arange(half_edge)[:, None]
    col_index = np.arange(length)[None, :]
    offset = (col_index - 2 * row_index).astype(np.float32)
    tap_offsets = np.arange(-4, 5).astype(np.float32)
    normalizer = np.sum(np.exp(-tap_offsets * tap_offsets / np.float32(4.5)), dtype=np.float32)
    taps = np.exp(-offset * offset / np.float32(4.5)) / normalizer
    weights = np.where(np.abs(offset) <= 4.0, taps, np.float32(0.0))
    return weights.astype(ml_dtypes.bfloat16).astype(np.float32)


def filter_tables(edge, snapshots):
    weights = smoother(edge)
    half = edge // 2
    table_x = np.kron(weights, np.eye(half, dtype=np.float32))
    table_y = np.stack(
        [np.kron(np.eye(half, dtype=np.float32), weights[:, h * half : (h + 1) * half]) for h in range(2)]
    )
    table_z = np.kron(weights.T, np.eye(snapshots, dtype=np.float32))
    as_bf16 = lambda a: a.astype(ml_dtypes.bfloat16)
    return as_bf16(table_x), as_bf16(table_y), as_bf16(table_z)


def dot(a, b):
    return jnp.dot(a, b, preferred_element_type=F32)


def filter_tile(tile, table_x, table_y, table_z):
    edge = tile.shape[0]
    half = edge // 2
    width = tile.shape[2]
    second = None
    for h in range(2):
        rows = tile[:, h * half : (h + 1) * half, :].reshape(edge * half, width)
        first = dot(table_x[...], rows).astype(BF16)
        term = dot(table_y[h], first)
        second = term if second is None else second + term
    return dot(second.astype(BF16), table_z[...]).astype(BF16)


def fold_gram(gram, snapshots):
    size = gram.shape[0]
    rows = lax.broadcasted_iota(jnp.int32, gram.shape, 0) // snapshots
    cols = lax.broadcasted_iota(jnp.int32, gram.shape, 1) // snapshots
    kept = jnp.where(rows == cols, gram, 0.0)
    strip = jnp.sum(kept.reshape(size // snapshots, snapshots, size), axis=0)
    folded = strip[:, :128]
    for start in range(128, size, 128):
        folded = folded + strip[:, start : start + 128]
    shift = 64
    while shift >= snapshots:
        folded = folded + pltpu.roll(folded, shift, axis=1)
        shift //= 2
    return folded


def factor_and_inverse(gram):
    order = gram.shape[0]
    rows = lax.broadcasted_iota(jnp.int32, gram.shape, 0)
    cols = lax.rem(lax.broadcasted_iota(jnp.int32, gram.shape, 1), order)
    rest = gram
    upper = jnp.zeros_like(gram)
    columns = []
    pivots = []
    for r in range(order):
        pivot = jnp.sqrt(rest[r : r + 1, r : r + 1])
        row = jnp.where(cols[:1] >= r, rest[r : r + 1, :] / pivot, 0.0)
        column = jnp.where(rows[:, :1] >= r, rest[:, r : r + 1] / pivot, 0.0)
        upper = jnp.where(rows == r, row, upper)
        columns.append(column)
        pivots.append(pivot)
        rest = rest - column * row
    inverse = jnp.zeros_like(gram)
    for r in range(order - 1, -1, -1):
        beyond = jnp.where(rows[:, :1] > r, columns[r], 0.0)
        unit = jnp.where(cols[:1] == r, 1.0, 0.0)
        row = (unit - jnp.sum(beyond * inverse, axis=0, keepdims=True)) / pivots[r]
        inverse = jnp.where(rows == r, row, inverse)
    return upper, inverse


class Sum:
    def __init__(self, axis, peers, buffer, send_sems, recv_sems):
        self.axis, self.peers, self.buffer = axis, peers, buffer
        self.send_sems, self.recv_sems = send_sems, recv_sems
        self.me = lax.axis_index(axis)

    def copy(self, peer, place):
        return pltpu.make_async_remote_copy(
            src_ref=self.buffer.at[self.me],
            dst_ref=self.buffer.at[place],
            send_sem=self.send_sems.at[peer],
            recv_sem=self.recv_sems.at[place],
            device_id={self.axis: peer},
            device_id_type=MESH,
        )

    def start(self, term):
        self.buffer[self.me] = term

        @pl.loop(1, self.peers)
        def _(step):
            self.copy(lax.rem(self.me + step, self.peers), self.me).start()

    def finish(self):
        @pl.loop(1, self.peers)
        def _(step):
            peer = lax.rem(self.me + step, self.peers)
            self.copy(peer, peer).wait_recv()

        total = self.buffer[0]
        for p in range(1, self.peers):
            total = total + self.buffer[p]

        @pl.loop(1, self.peers)
        def _(step):
            self.copy(lax.rem(self.me + step, self.peers), self.me).wait_send()

        return total


def split_inverse(inverse, parts, snapshots):
    size = parts.shape[1]
    wide = jnp.concatenate([inverse] * (size // 128), axis=1)
    tall = jnp.concatenate([wide] * (size // snapshots), axis=0)
    rows = lax.broadcasted_iota(jnp.int32, tall.shape, 0) // snapshots
    cols = lax.broadcasted_iota(jnp.int32, tall.shape, 1) // snapshots
    rest = jnp.where(rows == cols, tall, 0.0)
    for p in range(3):
        piece = rest.astype(BF16)
        parts[(2 - p) * size : (3 - p) * size, :] = piece
        rest = rest - piece.astype(F32)


def exchange_kernel(
    leaves, groups, snapshots, rows_all,
    tiles, routes_hbm, counts, table_x_hbm, table_y_hbm, table_z_hbm,
    factor_out, modes,
    routes, local, table_x, table_y, table_z, filtered, outgoing, relay, arrived, gram, parts, group_buf, leaf_buf,
    load_sems, table_sems, send_sems, recv_sems, relay_send, relay_recv,
    group_send, group_recv, leaf_send, leaf_recv,
):
    slots = tiles.shape[0]
    me = lax.axis_index("leaf")
    my_group = lax.axis_index("group")
    chips = leaves // 2
    far = chips // 2
    chip, core = me // 2, lax.rem(me, 2)

    loads = [
        pltpu.make_async_copy(src, dst, table_sems.at[n])
        for n, (src, dst) in enumerate(
            (
                (routes_hbm, routes),
                (table_x_hbm, table_x),
                (table_y_hbm, table_y),
                (table_z_hbm, table_z),
            )
        )
    ]
    loads += [pltpu.make_async_copy(tiles.at[t], local.at[t], load_sems.at[t]) for t in range(slots)]
    for copy in loads:
        copy.start()

    barrier = pltpu.get_barrier_semaphore()

    @pl.loop(1, leaves)
    def _(step):
        pl.semaphore_signal(
            barrier, inc=1, device_id={"leaf": lax.rem(me + step, leaves)}, device_id_type=MESH
        )

    @pl.loop(1, groups)
    def _(step):
        pl.semaphore_signal(
            barrier, inc=1, device_id={"group": lax.rem(my_group + step, groups)}, device_id_type=MESH
        )

    gram[...] = jnp.zeros_like(gram)
    for copy in loads:
        copy.wait()
    pl.semaphore_wait(barrier, leaves + groups - 2)

    def leaf_at(turn, flip):
        return lax.rem(chip + turn + chips, chips) * 2 + lax.rem(core + flip, 2)

    def dest_of(k):
        place = k + 2
        distance = far - place // 4
        m = lax.rem(place, 4)
        ahead = jnp.where(lax.rem(m, 2) == 0, distance, -distance)
        flip = jnp.where((m == 1) | (m == 2), 1, 0)
        half_way = k < 2
        near = k >= leaves - 2
        ahead = jnp.where(half_way, far, jnp.where(near, 0, ahead))
        flip = jnp.where(half_way, k, jnp.where(near, leaves - 1 - k, flip))
        return leaf_at(ahead, flip)

    def send(src, sender, sems, k, dest):
        return pltpu.make_async_remote_copy(
            src_ref=src,
            dst_ref=arrived.at[sender],
            send_sem=sems.at[k],
            recv_sem=recv_sems.at[sender],
            device_id={"leaf": dest},
            device_id_type=MESH,
        )

    def direct(k):
        return send(outgoing.at[k], me, send_sems, k, dest_of(k))

    def first_hop(k):
        return pltpu.make_async_remote_copy(
            src_ref=outgoing.at[k],
            dst_ref=relay.at[k],
            send_sem=send_sems.at[k],
            recv_sem=relay_recv.at[k],
            device_id={"leaf": leaf_at(1 - 2 * k, 0)},
            device_id_type=MESH,
        )

    def last_hops(k):
        sender = leaf_at(2 * k - 1, 0)
        return send(relay.at[k], sender, relay_send, k, leaf_at((far - 1) * (1 - 2 * k), k))

    count = counts[0]

    def slot_for(dest):
        slot = jnp.int32(0)
        found = jnp.int32(0)
        for t in range(slots):
            hit = jnp.where((routes[0, t] == dest) & (t < count), 1, 0)
            slot = slot + hit * t
            found = found + hit
        return slot, found > 0

    def prepare(k, block_of):
        slot, found = slot_for(dest_of(k))
        block = block_of(slot)
        outgoing[k] = jnp.where(found, block, jnp.zeros_like(block))

    early = 4
    for k in range(early):
        prepare(k, lambda slot: filter_tile(local[slot], table_x, table_y, table_z))
        (first_hop(k) if k < 2 else direct(k)).start()

    @pl.loop(0, slots)
    def _(t):
        block = filter_tile(local[t], table_x, table_y, table_z)
        block = jnp.where(t < count, block, jnp.zeros_like(block))
        filtered[t] = block
        gram[...] += lax.dot_general(
            block, block, (((0,), (0,)), ((), ())), preferred_element_type=F32
        )

    middle = 10

    @pl.loop(early, middle)
    def _(k):
        prepare(k, lambda slot: filtered[slot])
        direct(k).start()

    for k in range(2):
        first_hop(k).wait_recv()
        last_hops(k).start()

    group_sum = Sum("group", groups, group_buf, group_send, group_recv)
    group_sum.start(fold_gram(gram[...], snapshots))
    group_total = group_sum.finish()
    leaf_sum = Sum("leaf", leaves, leaf_buf, leaf_send, leaf_recv)
    leaf_sum.start(group_total)

    last = leaves - 1

    @pl.loop(middle, last)
    def _(k):
        prepare(k, lambda slot: filtered[slot])
        direct(k).start()

    prepare(last, lambda slot: filtered[slot])
    total = leaf_sum.finish()
    upper, inverse = factor_and_inverse(total / rows_all)
    factor_out[...] = upper[:, :snapshots]
    split_inverse(inverse, parts, snapshots)

    def apply(block):
        return dot(jnp.concatenate([block] * 3, axis=1), parts[...])

    modes[me] = apply(outgoing[last])

    @pl.loop(0, last)
    def _(n):
        k = jnp.where(n == 0, last - 1, jnp.where(n < 5, n + 1, jnp.where(n < 7, n - 5, n - 1)))
        source = dest_of(k)
        send(outgoing.at[0], source, send_sems, 0, source).wait_recv()
        modes[source] = apply(arrived[source])

    for k in range(2):
        first_hop(k).wait_send()
        last_hops(k).wait_send()

    @pl.loop(2, last)
    def _(k):
        direct(k).wait_send()


def exchange(tiles, routes, counts, leaves, groups, half, snapshots, rows_all):
    edge = tiles.shape[1]
    slots = tiles.shape[0]
    rows, cols = half * half, half * snapshots
    tables = filter_tables(edge, snapshots)
    vmem = pl.BlockSpec(memory_space=pltpu.VMEM)
    hbm = pl.BlockSpec(memory_space=pltpu.HBM)
    keep = lambda a: pltpu.with_memory_space_constraint(a, pltpu.HBM)
    return pl.pallas_call(
        functools.partial(exchange_kernel, leaves, groups, snapshots, rows_all),
        name="filter_exchange",
        out_shape=(
            jax.ShapeDtypeStruct((snapshots, snapshots), F32),
            jax.ShapeDtypeStruct((leaves, rows, cols), F32),
        ),
        in_specs=[hbm, hbm, pl.BlockSpec(memory_space=pltpu.SMEM), hbm, hbm, hbm],
        out_specs=(vmem, vmem),
        scratch_shapes=[
            pltpu.SMEM(routes.shape, jnp.int32),
            pltpu.VMEM((slots, edge, edge, edge * snapshots), BF16),
            *[pltpu.VMEM(t.shape, BF16) for t in tables],
            pltpu.VMEM((slots, rows, cols), BF16),
            pltpu.VMEM((leaves, rows, cols), BF16),
            pltpu.VMEM((2, rows, cols), BF16),
            pltpu.VMEM((leaves, rows, cols), BF16),
            pltpu.VMEM((cols, cols), F32),
            pltpu.VMEM((3 * cols, cols), BF16),
            pltpu.VMEM((groups, snapshots, 128), F32),
            pltpu.VMEM((leaves, snapshots, 128), F32),
            pltpu.SemaphoreType.DMA((slots,)),
            pltpu.SemaphoreType.DMA((4,)),
            pltpu.SemaphoreType.DMA((leaves,)),
            pltpu.SemaphoreType.DMA((leaves,)),
            pltpu.SemaphoreType.DMA((2,)),
            pltpu.SemaphoreType.DMA((2,)),
            pltpu.SemaphoreType.DMA((groups,)),
            pltpu.SemaphoreType.DMA((groups,)),
            pltpu.SemaphoreType.DMA((leaves,)),
            pltpu.SemaphoreType.DMA((leaves,)),
        ],
        compiler_params=pltpu.CompilerParams(
            collective_id=0, has_side_effects=True, vmem_limit_bytes=40 << 20
        ),
    )(keep(tiles), keep(routes), counts, *[keep(jnp.asarray(t)) for t in tables])


def shards(tile_fields, routes, counts):
    leaves = lax.axis_size("leaf")
    groups = lax.axis_size("group")
    slots, edge = tile_fields.shape[:2]
    snapshots = tile_fields.shape[3] // edge
    half = edge // 2
    rows_all = half**3 * slots * leaves * groups
    return exchange(
        tile_fields, routes, counts, leaves, groups, half, snapshots, float(rows_all)
    )


def solution(mesh):
    return jax.shard_map(
        shards,
        mesh=mesh,
        in_specs=(
            P(("leaf", "group"), None, None, None),
            P(("leaf", "group"), None),
            P(("leaf", "group")),
        ),
        out_specs=(P(), P(("leaf", "group"), None, None)),
        check_vma=False,
    )
```

time: 84.9 us -> 70.2 us (0.83)
  Pallas kernels: 73.8 us -> 66.2 us
  local copies, waits for them, and re-layouts: 9.4 us -> 2.61 us
    pallas_call x1 -> x0, Pallas kernels: 7.38 us -> none  [apply_inverse(): pl.pallas_call(functools.partial(apply_kernel, snapshots), name='apply_in...]
    unnamed x16 -> x2, local copies, waits for them, and re-layouts: 9.4 us -> 2.61 us
where the time goes in v2:
time: 70.2 us; the launch traced here: 70.1 us
  Pallas kernels  66.2 us (94%)
  local copies, waits for them, and re-layouts  2.61 us (4%)
  between operations  1.28 us (2%)
    pallas_call x1, Pallas kernels, exchange(): pl.pallas_call(functools.partial(exchange_kernel, leaves, groups, snapsho...  66.2 us
    unnamed x2, local copies, waits for them, and re-layouts  2.61 us

profile of v2, /device:TPU:1, one launch (start us, length us, event | category | flops | bytes accessed | tf_op | source)
XLA Modules:
  0.0 70.1 jit_solution(14222377635888435827)
XLA Ops:
  1.3 66.2 %filter_exchange.1 = (f32[16,16]{1,0:T(8,128)S(1)}, f32[16,256,256]{2,1,0:T(8,128)S(1)}) custom-call(bf16[8,32,32,512]{3,2,1,0:T(8,128)(2,1)} %tiles.1, s32[1,8]{1,0:T(1,128)} %routes_hbm.1, s32[1]{0:T(128)S(6)} %copy.10.counts, bf16[256,512]{1,0:T(8,128)(2,1)} %constant.6.clone.table_x_hbm, bf16[2,256,256]{2,1,0:T(8,128)(2,1)} %constant.7.clone.table_y_hbm, ...), custom_call_target="tpu_custom_call" | custom-call | tf_op jit(solution)/shard_map/filter_exchange/pallas_call | solution.py:332
  67.5 0.6 copy.11
  68.1 2.0 %copy.12 = f32[16,256,256]{2,1,0:T(8,128)} copy(f32[16,256,256]{2,1,0:T(8,128)S(1)} %get-tuple-element.5) | data formatting | bytes 8388608

commit v3 on v2

--- a/solution.py
+++ b/solution.py
@@ -257,9 +257,18 @@
         outgoing[k] = jnp.where(found, block, jnp.zeros_like(block))
 
     early = 4
-    for k in range(early):
+
+    @pl.loop(0, early)
+    def _(k):
         prepare(k, lambda slot: filter_tile(local[slot], table_x, table_y, table_z))
-        (first_hop(k) if k < 2 else direct(k)).start()
+
+        @pl.when(k < 2)
+        def _():
+            first_hop(k).start()
+
+        @pl.when(k >= 2)
+        def _():
+            direct(k).start()
 
     @pl.loop(0, slots)
     def _(t):
@@ -270,33 +279,27 @@
             block, block, (((0,), (0,)), ((), ())), preferred_element_type=F32
         )
 
-    middle = 10
-
-    @pl.loop(early, middle)
-    def _(k):
-        prepare(k, lambda slot: filtered[slot])
-        direct(k).start()
-
+    leaf_sum = Sum("leaf", leaves, leaf_buf, leaf_send, leaf_recv)
+    leaf_sum.start(fold_gram(gram[...], snapshots))
+    last = leaves - 1
+    near = last - 5
+
+    def send_blocks(first, end):
+        @pl.loop(first, end)
+        def _(k):
+            prepare(k, lambda slot: filtered[slot])
+            direct(k).start()
+
+    send_blocks(early, near)
     for k in range(2):
         first_hop(k).wait_recv()
         last_hops(k).start()
+    send_blocks(near, last)
+    prepare(last, lambda slot: filtered[slot])
 
     group_sum = Sum("group", groups, group_buf, group_send, group_recv)
-    group_sum.start(fold_gram(gram[...], snapshots))
-    group_total = group_sum.finish()
-    leaf_sum = Sum("leaf", leaves, leaf_buf, leaf_send, leaf_recv)
-    leaf_sum.start(group_total)
-
-    last = leaves - 1
-
-    @pl.loop(middle, last)
-    def _(k):
-        prepare(k, lambda slot: filtered[slot])
-        direct(k).start()
-
-    prepare(last, lambda slot: filtered[slot])
-    total = leaf_sum.finish()
-    upper, inverse = factor_and_inverse(total / rows_all)
+    group_sum.start(leaf_sum.finish())
+    upper, inverse = factor_and_inverse(group_sum.finish() / rows_all)
     factor_out[...] = upper[:, :snapshots]
     split_inverse(inverse, parts, snapshots)
 
@@ -307,7 +310,8 @@
 
     @pl.loop(0, last)
     def _(n):
-        k = jnp.where(n == 0, last - 1, jnp.where(n < 5, n + 1, jnp.where(n < 7, n - 5, n - 1)))
+        k = jnp.where(n < near - 1, n + 1, jnp.where(n < near + 1, n - near + 1, n - 1))
+        k = jnp.where(n == 0, last - 1, k)
         source = dest_of(k)
         send(outgoing.at[0], source, send_sems, 0, source).wait_recv()
         modes[source] = apply(arrived[source])
@@ -367,6 +371,39 @@
     )(keep(tiles), keep(routes), counts, *[keep(jnp.asarray(t)) for t in tables])
 
 
+def store_kernel(factor, modes, factor_out, modes_out, sems):
+    pieces = sems.shape[0] - 1
+    size = modes.shape[0] // pieces
+    copies = [
+        pltpu.make_async_copy(
+            modes.at[pl.ds(p * size, size)], modes_out.at[pl.ds(p * size, size)], sems.at[p]
+        )
+        for p in range(pieces)
+    ]
+    copies.append(pltpu.make_async_copy(factor, factor_out, sems.at[pieces]))
+    for copy in copies:
+        copy.start()
+    for copy in copies:
+        copy.wait()
+
+
+def store(factor, modes):
+    vmem = pl.BlockSpec(memory_space=pltpu.VMEM)
+    hbm = pl.BlockSpec(memory_space=pltpu.HBM)
+    return pl.pallas_call(
+        store_kernel,
+        name="store",
+        out_shape=(
+            jax.ShapeDtypeStruct(factor.shape, factor.dtype),
+            jax.ShapeDtypeStruct(modes.shape, modes.dtype),
+        ),
+        in_specs=[vmem, vmem],
+        out_specs=(hbm, hbm),
+        scratch_shapes=[pltpu.SemaphoreType.DMA((5,))],
+        compiler_params=pltpu.CompilerParams(vmem_limit_bytes=16 << 20),
+    )(factor, modes)
+
+
 def shards(tile_fields, routes, counts):
     leaves = lax.axis_size("leaf")
     groups = lax.axis_size("group")
@@ -374,9 +411,10 @@
     snapshots = tile_fields.shape[3] // edge
     half = edge // 2
     rows_all = half**3 * slots * leaves * groups
-    return exchange(
+    factor, modes = exchange(
         tile_fields, routes, counts, leaves, groups, half, snapshots, float(rows_all)
     )
+    return store(factor, modes)
 
 
 def solution(mesh):

time: 70.2 us -> 67.6 us (0.963)
  local copies, waits for them, and re-layouts: 2.61 us -> 0 us
    unnamed x2 -> x0, local copies, waits for them, and re-layouts: 2.61 us -> none
    pallas_call x0 -> x1, Pallas kernels: none -> 2.05 us  [store(): pl.pallas_call(store_kernel, name='store', out_shape=(jax.ShapeDtypeStruc...]
    pallas_call x1, Pallas kernels: 66.2 us -> 64.2 us  [exchange(): pl.pallas_call(functools.partial(exchange_kernel, leaves, groups, snapsho...]
where the time goes in v3:
time: 67.6 us; the launch traced here: 67.5 us
  Pallas kernels  66.2 us (98%)
  between operations  1.28 us (2%)
    pallas_call x1, Pallas kernels, exchange(): pl.pallas_call(functools.partial(exchange_kernel, leaves, groups, snapsho...  64.2 us
    pallas_call x1, Pallas kernels, store(): pl.pallas_call(store_kernel, name='store', out_shape=(jax.ShapeDtypeStruc...  2.05 us

profile of v3, /device:TPU:1, one launch (start us, length us, event | category | flops | bytes accessed | tf_op | source)
XLA Modules:
  0.0 67.5 jit_solution(5368438920197067311)
XLA Ops:
  1.3 64.2 %filter_exchange.1 = (f32[16,16]{1,0:T(8,128)S(1)}, f32[16,256,256]{2,1,0:T(8,128)S(1)}) custom-call(bf16[8,32,32,512]{3,2,1,0:T(8,128)(2,1)} %tiles.1, s32[1,8]{1,0:T(1,128)} %routes_hbm.1, s32[1]{0:T(128)S(6)} %copy.8.counts, bf16[256,512]{1,0:T(8,128)(2,1)} %constant.6.clone.table_x_hbm, bf16[2,256,256]{2,1,0:T(8,128)(2,1)} %constant.7.clone.table_y_hbm, ...), custom_call_target="tpu_custom_call" | custom-call | tf_op jit(solution)/shard_map/filter_exchange/pallas_call | solution.py:336
  65.5 2.1 %store.1 = (f32[16,16]{1,0:T(8,128)}, f32[16,256,256]{2,1,0:T(8,128)}) custom-call(f32[16,16]{1,0:T(8,128)S(1)} %get-tuple-element.4.factor, f32[16,256,256]{2,1,0:T(8,128)S(1)} %get-tuple-element.5.modes), custom_call_target="tpu_custom_call" | custom-call | tf_op jit(solution)/shard_map/store/pallas_call | solution.py:393
